TPU v7x, 32 devices: a whole 2x2x4 slice. The times are simulated.
32 devices in a mesh: dp: 4 (over y, x), seq: 8 (over z, core).
Axes of the slice: x: 2, y: 2, z: 4, core: 2. Of those that a mesh axis runs over, the one named last changes fastest.
Arguments:
- tokens: bfloat16 [4, 4, 512, 1024], P('dp', None, 'seq'), may hold values from -6 to 6
- norm1_gain: bfloat16 [1024], P('dp'), may hold values from 0.5 to 1.5
- w_query: bfloat16 [1024, 1024], P('dp'), may hold values from -0.1875 to 0.1875
- w_latent: bfloat16 [1024, 512], P('dp'), may hold values from -0.1875 to 0.1875
- w_key_up: bfloat16 [256, 1024], P('dp'), may hold values from -0.375 to 0.375
- w_value_up: bfloat16 [256, 1024], P('dp'), may hold values from -0.375 to 0.375
- w_out: bfloat16 [1024, 1024], P('dp'), may hold values from -1.5 to 1.5
- norm2_gain: bfloat16 [1024], P('dp'), may hold values from 0.5 to 1.5
- w_gate: bfloat16 [1024, 2816], P('dp'), may hold values from -0.1875 to 0.1875
- w_up: bfloat16 [1024, 2816], P('dp'), may hold values from -0.1875 to 0.1875
- w_down: bfloat16 [2816, 1024], P('dp'), may hold values from -0.109375 to 0.109375
- out_grad: bfloat16 [4, 4, 512, 1024], P('dp', None, 'seq'), may hold values from -6 to 6
- seq_lengths: int32 [4, 66], P('dp'), may hold values from 0 to 1024, as said below
Outputs:
- layer_out: bfloat16 [4, 4, 512, 1024], P('dp', None, 'seq')
- tokens_grad: bfloat16 [4, 4, 512, 1024], P('dp', None, 'seq')
- norm1_gain_grad: float32 [1024], P('dp')
- w_query_grad: float32 [1024, 1024], P('dp')
- w_latent_grad: float32 [1024, 512], P('dp')
- w_key_up_grad: float32 [256, 1024], P('dp')
- w_value_up_grad: float32 [256, 1024], P('dp')
- w_out_grad: float32 [1024, 1024], P('dp')
- norm2_gain_grad: float32 [1024], P('dp')
- w_gate_grad: float32 [1024, 2816], P('dp')
- w_up_grad: float32 [1024, 2816], P('dp')
- w_down_grad: float32 [2816, 1024], P('dp')
Inputs may be any that keep to these rules, and one draw needn't show every extreme that they name: `seq_lengths`: the entries of a stream sum to 2048. Even entries are sequence lengths; every stream holds one sequence of exactly 1024 positions. Odd entries are padding of at most 64 positions.
All inputs are finite; a program needn't handle non-finite values.
Results may differ from a plain program's by a relative error of at most 0.02.
Values may be sent and summed in bfloat16 or wider, within the bound.
No kernel may reach another device: no remote copies, remote signals or barrier semaphores. Data moves between devices by JAX's collectives and lax.ppermute only.
A program may use at most 256 MiB of HBM per device.

v0:
```python
import math
import jax
import jax.numpy as jnp
from jax import lax
from jax.sharding import PartitionSpec as P

HEADS = 16
HEAD_DIM = 64
GROUPS = 2
LATENT = 256
SEQ_MIN = 1024
NEG_FILL = -1e30
NORM_EPS = 1e-05


def rms_scale(values, gain):
    inverse = lax.rsqrt(jnp.mean(values * values, axis=-1, keepdims=True) + NORM_EPS)
    return values * inverse * gain


def swish_product(gate_vals, up_vals):
    return gate_vals * jax.nn.sigmoid(gate_vals) * up_vals


def seq_table(stretches):
    run_ends = jnp.cumsum(stretches)
    firsts = run_ends - stretches
    return (firsts[0::2], stretches[0::2])


def inside_table(starts, lengths, positions):
    return (positions[:, None] >= starts[None, :]) & (
        positions[:, None] < starts[None, :] + lengths[None, :]
    )


def label_rows(inside):
    labels = jnp.arange(1, inside.shape[1] + 1, dtype=jnp.int32)
    return jnp.sum(jnp.where(inside, labels[None, :], 0), axis=1)


def per_device(
    tokens,
    norm1_gain,
    w_query,
    w_latent,
    w_key_up,
    w_value_up,
    w_out,
    norm2_gain,
    w_gate,
    w_up,
    w_down,
    out_grad,
    seq_lengths,
):
    gathered = (
        lax.all_gather(norm1_gain, "dp", axis=0, tiled=True),
        lax.all_gather(w_query, "dp", axis=0, tiled=True),
        lax.all_gather(w_latent, "dp", axis=0, tiled=True),
        lax.all_gather(w_key_up, "dp", axis=0, tiled=True),
        lax.all_gather(w_value_up, "dp", axis=0, tiled=True),
        lax.all_gather(w_out, "dp", axis=0, tiled=True),
        lax.all_gather(norm2_gain, "dp", axis=0, tiled=True),
        lax.all_gather(w_gate, "dp", axis=0, tiled=True),
        lax.all_gather(w_up, "dp", axis=0, tiled=True),
        lax.all_gather(w_down, "dp", axis=0, tiled=True),
    )
    gain_one, query_w, latent_w, key_w, value_w, out_w, gain_two, gate_w, up_w, down_w = gathered
    piece_count = tokens.shape[1]
    block_rows = tokens.shape[2]
    row_width = tokens.shape[3]
    tok_rows = piece_count * block_rows
    my_index = lax.axis_index("seq")
    span_rows = block_rows * lax.axis_size("seq")
    longest = max(SEQ_MIN, span_rows)
    window = longest + block_rows
    stream_len = piece_count * span_rows
    latent_width = GROUPS * LATENT
    per_group = HEADS // GROUPS
    score_scale = 1.0 / math.sqrt(HEAD_DIM)
    seq_first, seq_len = seq_table(seq_lengths[0])
    row_pos = (
        jnp.arange(piece_count, dtype=jnp.int32)[:, None] * span_rows
        + my_index * block_rows
        + jnp.arange(block_rows, dtype=jnp.int32)[None, :]
    )
    row_labels = label_rows(inside_table(seq_first, seq_len, row_pos.reshape(-1))).reshape(
        piece_count, block_rows
    )
    key_first = jnp.maximum(row_pos[:, 0] + block_rows - window, 0)
    key_pos = key_first[:, None] + jnp.arange(window, dtype=jnp.int32)[None, :]
    key_labels = label_rows(inside_table(seq_first, seq_len, key_pos.reshape(-1))).reshape(
        piece_count, window
    )
    same_seq = (
        (row_labels[:, :, None] == key_labels[:, None, :])
        & (row_labels[:, :, None] > 0)
        & (key_pos[:, None, :] <= row_pos[:, :, None])
    )
    masks = same_seq | (key_pos[:, None, :] == row_pos[:, :, None])

    def windows_of(stream_vals):
        return jnp.stack(
            [
                lax.dynamic_slice_in_dim(stream_vals, key_first[piece_id], window, 0)
                for piece_id in range(piece_count)
            ]
        )

    tok_float = tokens[0].reshape(tok_rows, row_width).astype(jnp.float32)
    gain_one_f = gain_one.astype(jnp.float32)
    gain_two_f = gain_two.astype(jnp.float32)
    normed = rms_scale(tok_float, gain_one_f).astype(jnp.bfloat16)
    queries = jnp.dot(normed, query_w, preferred_element_type=jnp.float32).astype(jnp.bfloat16)
    latent = jnp.dot(normed, latent_w, preferred_element_type=jnp.float32).astype(jnp.bfloat16)
    key_up = key_w.reshape(LATENT, HEADS, HEAD_DIM)
    value_up = value_w.reshape(LATENT, HEADS, HEAD_DIM)
    query_heads = queries.reshape(tok_rows, HEADS, HEAD_DIM)
    absorbed = jnp.einsum(
        "thd,chd->thc", query_heads, key_up, preferred_element_type=jnp.float32
    ).astype(jnp.bfloat16)
    absorbed_p = absorbed.reshape(piece_count, block_rows, HEADS, LATENT)
    latent_pieces = latent.reshape(piece_count, block_rows, latent_width)
    whole_stream = lax.all_gather(latent_pieces, "seq", axis=1, tiled=True).reshape(
        stream_len, latent_width
    )
    key_blocks = windows_of(whole_stream)

    def group_scores(keys_p, group_id):
        head_span = slice(group_id * per_group, (group_id + 1) * per_group)
        group_queries = absorbed_p[:, :, head_span, :]
        group_keys = keys_p[:, :, group_id * LATENT : (group_id + 1) * LATENT]
        scores = (
            jnp.einsum(
                "pthc,pkc->pthk", group_queries, group_keys, preferred_element_type=jnp.float32
            )
            * score_scale
        )
        return (group_queries, group_keys, jnp.where(masks[:, :, None, :], scores, NEG_FILL))

    log_parts = []
    mixed_parts = []
    for group_id in range(GROUPS):
        group_keys, scores = group_scores(key_blocks, group_id)[1:]
        row_top = jnp.max(scores, axis=-1)
        group_log = row_top + jnp.log(jnp.sum(jnp.exp(scores - row_top[..., None]), axis=-1))
        prob_vals = jnp.exp(scores - group_log[..., None]).astype(jnp.bfloat16)
        mixed_parts.append(
            jnp.einsum("pthk,pkc->pthc", prob_vals, group_keys, preferred_element_type=jnp.float32)
        )
        log_parts.append(group_log)
    log_total = jnp.concatenate(log_parts, axis=2)
    mixed_latent = jnp.concatenate(mixed_parts, axis=2).reshape(tok_rows, HEADS, LATENT)
    mixed_round = mixed_latent.astype(jnp.bfloat16)
    heads_out = (
        jnp.einsum("thc,chd->thd", mixed_round, value_up, preferred_element_type=jnp.float32)
        .astype(jnp.bfloat16)
        .reshape(tok_rows, HEADS * HEAD_DIM)
    )
    resid = tok_float + jnp.dot(heads_out, out_w, preferred_element_type=jnp.float32)
    normed_two = rms_scale(resid, gain_two_f).astype(jnp.bfloat16)
    gate_vals = jnp.dot(normed_two, gate_w, preferred_element_type=jnp.float32)
    up_vals = jnp.dot(normed_two, up_w, preferred_element_type=jnp.float32)
    hidden = swish_product(gate_vals, up_vals).astype(jnp.bfloat16)
    layer_out = (resid + jnp.dot(hidden, down_w, preferred_element_type=jnp.float32)).astype(
        jnp.bfloat16
    )
    grad_round = out_grad[0].reshape(tok_rows, row_width)
    grad_float = grad_round.astype(jnp.float32)
    down_grad = jnp.einsum("tf,td->fd", hidden, grad_round, preferred_element_type=jnp.float32)
    d_hidden = jnp.einsum("td,fd->tf", grad_round, down_w, preferred_element_type=jnp.float32)
    swish_pull = jax.vjp(swish_product, gate_vals, up_vals)[1]
    d_gate, d_up = swish_pull(d_hidden)
    d_gate = d_gate.astype(jnp.bfloat16)
    d_up = d_up.astype(jnp.bfloat16)
    gate_grad = jnp.einsum("td,tf->df", normed_two, d_gate, preferred_element_type=jnp.float32)
    up_grad = jnp.einsum("td,tf->df", normed_two, d_up, preferred_element_type=jnp.float32)
    d_normed_two = jnp.einsum(
        "tf,df->td", d_gate, gate_w, preferred_element_type=jnp.float32
    ) + jnp.einsum("tf,df->td", d_up, up_w, preferred_element_type=jnp.float32)
    norm_two_pull = jax.vjp(rms_scale, resid, gain_two_f)[1]
    d_resid_norm, gain_two_grad = norm_two_pull(d_normed_two)
    d_resid = grad_float + d_resid_norm
    d_resid_round = d_resid.astype(jnp.bfloat16)
    out_w_grad = jnp.einsum(
        "te,td->ed", heads_out, d_resid_round, preferred_element_type=jnp.float32
    )
    d_heads = (
        jnp.einsum("td,ed->te", d_resid_round, out_w, preferred_element_type=jnp.float32)
        .astype(jnp.bfloat16)
        .reshape(tok_rows, HEADS, HEAD_DIM)
    )
    value_grad = jnp.einsum(
        "thc,thd->chd", mixed_round, d_heads, preferred_element_type=jnp.float32
    ).reshape(LATENT, HEADS * HEAD_DIM)
    d_mixed = jnp.einsum(
        "thd,chd->thc", d_heads, value_up, preferred_element_type=jnp.float32
    ).astype(jnp.bfloat16)
    delta = jnp.sum(d_mixed.astype(jnp.float32) * mixed_latent, axis=-1)
    d_mixed_p = d_mixed.reshape(piece_count, block_rows, HEADS, LATENT)
    delta_p = delta.reshape(piece_count, block_rows, HEADS)
    again_stream = lax.all_gather(latent_pieces, "seq", axis=1, tiled=True).reshape(
        stream_len, latent_width
    )
    back_blocks = windows_of(again_stream)
    absorbed_parts = []
    key_parts = []
    for group_id in range(GROUPS):
        head_span = slice(group_id * per_group, (group_id + 1) * per_group)
        group_queries, group_keys, scores = group_scores(back_blocks, group_id)
        prob_vals = jnp.exp(scores - log_total[:, :, head_span, None])
        group_grads = d_mixed_p[:, :, head_span, :]
        d_probs = jnp.einsum(
            "pthc,pkc->pthk", group_grads, group_keys, preferred_element_type=jnp.float32
        )
        d_scores = (prob_vals * (d_probs - delta_p[:, :, head_span, None])).astype(jnp.bfloat16)
        absorbed_parts.append(
            jnp.einsum("pthk,pkc->pthc", d_scores, group_keys, preferred_element_type=jnp.float32)
        )
        key_terms = score_scale * jnp.einsum(
            "pthk,pthc->pkc", d_scores, group_queries, preferred_element_type=jnp.float32
        )
        key_terms = key_terms + jnp.einsum(
            "pthk,pthc->pkc",
            prob_vals.astype(jnp.bfloat16),
            group_grads,
            preferred_element_type=jnp.float32,
        )
        key_parts.append(key_terms)
    d_abs_sum = jnp.concatenate(absorbed_parts, axis=2).reshape(tok_rows, HEADS, LATENT)
    window_grads = jnp.concatenate(key_parts, axis=2)
    grad_term = jnp.zeros((stream_len, latent_width), jnp.float32)
    for piece_id in range(piece_count):
        current = lax.dynamic_slice_in_dim(grad_term, key_first[piece_id], window, 0)
        grad_term = lax.dynamic_update_slice_in_dim(
            grad_term, current + window_grads[piece_id], key_first[piece_id], 0
        )
    latent_total = lax.psum_scatter(
        grad_term.reshape(piece_count, span_rows, latent_width),
        "seq",
        scatter_dimension=1,
        tiled=True,
    ).reshape(tok_rows, latent_width)
    d_absorbed = (score_scale * d_abs_sum).astype(jnp.bfloat16)
    key_grad = jnp.einsum(
        "thc,thd->chd", d_absorbed, query_heads, preferred_element_type=jnp.float32
    ).reshape(LATENT, HEADS * HEAD_DIM)
    d_queries = (
        jnp.einsum("thc,chd->thd", d_absorbed, key_up, preferred_element_type=jnp.float32)
        .astype(jnp.bfloat16)
        .reshape(tok_rows, HEADS * HEAD_DIM)
    )
    d_latent = latent_total.astype(jnp.bfloat16)
    query_grad = jnp.einsum("td,te->de", normed, d_queries, preferred_element_type=jnp.float32)
    latent_grad = jnp.einsum("td,te->de", normed, d_latent, preferred_element_type=jnp.float32)
    d_normed = jnp.einsum(
        "te,de->td", d_queries, query_w, preferred_element_type=jnp.float32
    ) + jnp.einsum("te,de->td", d_latent, latent_w, preferred_element_type=jnp.float32)
    norm_one_pull = jax.vjp(rms_scale, tok_float, gain_one_f)[1]
    d_tok_norm, gain_one_grad = norm_one_pull(d_normed)
    tokens_grad = (d_resid + d_tok_norm).astype(jnp.bfloat16)
    grads = (
        gain_one_grad,
        query_grad,
        latent_grad,
        key_grad,
        value_grad,
        out_w_grad,
        gain_two_grad,
        gate_grad,
        up_grad,
        down_grad,
    )
    shares = (
        lax.psum_scatter(
            grads[0].astype(jnp.bfloat16), "dp", scatter_dimension=0, tiled=True
        ).astype(jnp.float32),
        lax.psum_scatter(
            grads[1].astype(jnp.bfloat16), "dp", scatter_dimension=0, tiled=True
        ).astype(jnp.float32),
        lax.psum_scatter(
            grads[2].astype(jnp.bfloat16), "dp", scatter_dimension=0, tiled=True
        ).astype(jnp.float32),
        lax.psum_scatter(
            grads[3].astype(jnp.bfloat16), "dp", scatter_dimension=0, tiled=True
        ).astype(jnp.float32),
        lax.psum_scatter(
            grads[4].astype(jnp.bfloat16), "dp", scatter_dimension=0, tiled=True
        ).astype(jnp.float32),
        lax.psum_scatter(
            grads[5].astype(jnp.bfloat16), "dp", scatter_dimension=0, tiled=True
        ).astype(jnp.float32),
        lax.psum_scatter(
            grads[6].astype(jnp.bfloat16), "dp", scatter_dimension=0, tiled=True
        ).astype(jnp.float32),
        lax.psum_scatter(
            grads[7].astype(jnp.bfloat16), "dp", scatter_dimension=0, tiled=True
        ).astype(jnp.float32),
        lax.psum_scatter(
            grads[8].astype(jnp.bfloat16), "dp", scatter_dimension=0, tiled=True
        ).astype(jnp.float32),
        lax.psum_scatter(
            grads[9].astype(jnp.bfloat16), "dp", scatter_dimension=0, tiled=True
        ).astype(jnp.float32),
    )
    summed = lax.psum(
        (
            shares[0],
            shares[1],
            shares[2],
            shares[3],
            shares[4],
            shares[5],
            shares[6],
            shares[7],
            shares[8],
            shares[9],
        ),
        "seq",
    )
    return (
        layer_out.reshape(1, piece_count, block_rows, row_width),
        tokens_grad.reshape(1, piece_count, block_rows, row_width),
        summed[0],
        summed[1],
        summed[2],
        summed[3],
        summed[4],
        summed[5],
        summed[6],
        summed[7],
        summed[8],
        summed[9],
    )


def solution(mesh):
    in_specs = (
        P("dp", None, "seq", None),
        P("dp"),
        P("dp", None),
        P("dp", None),
        P("dp", None),
        P("dp", None),
        P("dp", None),
        P("dp"),
        P("dp", None),
        P("dp", None),
        P("dp", None),
        P("dp", None, "seq", None),
        P("dp", None),
    )
    out_specs = (
        P("dp", None, "seq", None),
        P("dp", None, "seq", None),
        P("dp"),
        P("dp", None),
        P("dp", None),
        P("dp", None),
        P("dp", None),
        P("dp", None),
        P("dp"),
        P("dp", None),
        P("dp", None),
        P("dp", None),
    )
    return jax.shard_map(
        per_device, mesh=mesh, in_specs=in_specs, out_specs=out_specs, check_vma=False
    )
```

profile of v0, /device:TPU:0, one launch (start us, length us, event | category | flops | bytes accessed | tf_op | source)
XLA Modules:
  0.0 1120.6 jit_solution(5432038570921758720)
XLA Ops:
  11.3 9.5 all-gather
  22.1 17.1 %all-gather.12.cloned.1.call-done = bf16[1024,512]{1,0:T(8,128)(2,1)} async-done(((bf16[256,512]{1,0:T(8,128)(2,1)}), bf16[1024,512]{1,0:T(8,128)(2,1)}) %all-gather.12.cloned.1.call-update) | async-done | bytes 1048592 | tf_op jit(solution)/shard_map/all_gather | solution.py:60
  46.3 14.0 %all_gather.36 = bf16[256,1024]{1,0:T(8,128)(2,1)S(1)} all-gather(bf16[64,1024]{1,0:T(8,128)(2,1)S(1)} %copy-done.40), channel_id=1, replica_groups=mesh['dp'=4,'seq'=8] {'dp'}, dimensions={0}, use_global_device_ids=true | all-gather | bytes 655360 | tf_op jit(solution)/shard_map/all_gather | solution.py:61
  60.8 12.0 %all_gather.39 = bf16[256,1024]{1,0:T(8,128)(2,1)S(1)} all-gather(bf16[64,1024]{1,0:T(8,128)(2,1)S(1)} %copy-done.41), channel_id=1, replica_groups=mesh['dp'=4,'seq'=8] {'dp'}, dimensions={0}, use_global_device_ids=true | all-gather | bytes 655360 | tf_op jit(solution)/shard_map/all_gather | solution.py:62
  79.2 8.8 all-gather.1
  94.2 18.0 %all-gather.14.cloned.1.call-done = bf16[4,512,512]{2,1,0:T(8,128)(2,1)} async-done(((bf16[4,64,512]{2,1,0:T(8,128)(2,1)}), bf16[4,512,512]{2,1,0:T(8,128)(2,1)}) %all-gather.14.cloned.1.call-update) | async-done | bytes 2097168 | tf_op jit(solution)/shard_map/all_gather | solution.py:125
  140.6 8.2 all-gather.16.cloned.1.call-done
  151.4 64.9 %all-gather.18.cloned.1.call-done = bf16[1024,2816]{1,0:T(8,128)(2,1)} async-done(((bf16[256,2816]{1,0:T(8,128)(2,1)}), bf16[1024,2816]{1,0:T(8,128)(2,1)}) %all-gather.18.cloned.1.call-update) | async-done | bytes 5767184 | tf_op jit(solution)/shard_map/all_gather | solution.py:65
  222.2 61.7 %all-gather.20.cloned.1.call-done = bf16[1024,2816]{1,0:T(8,128)(2,1)} async-done(((bf16[256,2816]{1,0:T(8,128)(2,1)}), bf16[1024,2816]{1,0:T(8,128)(2,1)}) %all-gather.20.cloned.1.call-update) | async-done | bytes 5767184 | tf_op jit(solution)/shard_map/all_gather | solution.py:66
  289.7 61.8 %all-gather.22.cloned.1.call-done = bf16[2816,1024]{1,0:T(8,128)(2,1)} async-done(((bf16[704,1024]{1,0:T(8,128)(2,1)}), bf16[2816,1024]{1,0:T(8,128)(2,1)}) %all-gather.22.cloned.1.call-update) | async-done | bytes 5767184 | tf_op jit(solution)/shard_map/all_gather | solution.py:67
  351.5 9.5 multiply_convert_fusion.2
  377.9 6.8 multiply_convert_fusion
  391.0 8.1 bitcast_add_fusion
  411.4 7.5 bitcast_add_fusion.1
  485.7 23.7 %reduce-scatter.10.cloned.1.call-done = f32[4,64,512]{2,1,0:T(8,128)} async-done(((f32[4,512,512]{2,1,0:T(8,128)}), f32[4,64,512]{2,1,0:T(8,128)}) %reduce-scatter.10.cloned.1.call-update) | async-done | bytes 524304 | tf_op jit(solution)/shard_map/reduce_scatter | solution.py:239
  540.9 22.0 %reduce-scatter.16.cloned.1.call-done = bf16[64,1024]{1,0:T(8,128)(2,1)} async-done(((bf16[256,1024]{1,0:T(8,128)(2,1)}), bf16[64,1024]{1,0:T(8,128)(2,1)}) %reduce-scatter.16.cloned.1.call-update) | async-done | bytes 131088 | tf_op jit(solution)/shard_map/reduce_scatter | solution.py:285
  562.8 38.8 %reduce-scatter.20.cloned.1.call-done = bf16[256,1024]{1,0:T(8,128)(2,1)} async-done(((bf16[1024,1024]{1,0:T(8,128)(2,1)}), bf16[256,1024]{1,0:T(8,128)(2,1)}) %reduce-scatter.20.cloned.1.call-update) | async-done | bytes 524304 | tf_op jit(solution)/shard_map/reduce_scatter | solution.py:291
  601.6 38.9 %reduce-scatter.12.cloned.1.call-done = bf16[256,1024]{1,0:T(8,128)(2,1)} async-done(((bf16[1024,1024]{1,0:T(8,128)(2,1)}), bf16[256,1024]{1,0:T(8,128)(2,1)}) %reduce-scatter.12.cloned.1.call-update) | async-done | bytes 524304 | tf_op jit(solution)/shard_map/reduce_scatter | solution.py:279
  642.7 8.9 all-reduce.3
  652.8 18.3 %reduce-scatter.14.cloned.1.call-done = bf16[256,512]{1,0:T(8,128)(2,1)} async-done(((bf16[1024,512]{1,0:T(8,128)(2,1)}), bf16[256,512]{1,0:T(8,128)(2,1)}) %reduce-scatter.14.cloned.1.call-update) | async-done | bytes 262160 | tf_op jit(solution)/shard_map/reduce_scatter | solution.py:282
  671.1 69.0 %reduce-scatter.22.cloned.1.call-done = bf16[256,2816]{1,0:T(8,128)(2,1)} async-done(((bf16[1024,2816]{1,0:T(8,128)(2,1)}), bf16[256,2816]{1,0:T(8,128)(2,1)}) %reduce-scatter.22.cloned.1.call-update) | async-done | bytes 1441808 | tf_op jit(solution)/shard_map/reduce_scatter | solution.py:297
  740.1 68.9 %reduce-scatter.24.cloned.1.call-done = bf16[256,2816]{1,0:T(8,128)(2,1)} async-done(((bf16[1024,2816]{1,0:T(8,128)(2,1)}), bf16[256,2816]{1,0:T(8,128)(2,1)}) %reduce-scatter.24.cloned.1.call-update) | async-done | bytes 1441808 | tf_op jit(solution)/shard_map/reduce_scatter | solution.py:300
  809.1 68.9 %reduce-scatter.26.cloned.1.call-done = bf16[704,1024]{1,0:T(8,128)(2,1)} async-done(((bf16[2816,1024]{1,0:T(8,128)(2,1)}), bf16[704,1024]{1,0:T(8,128)(2,1)}) %reduce-scatter.26.cloned.1.call-update) | async-done | bytes 1441808 | tf_op jit(solution)/shard_map/reduce_scatter | solution.py:303
  878.0 235.7 %all-reduce.5 = (f32[256]{0:T(256)}, f32[256,1024]{1,0:T(8,128)}, f32[256,512]{1,0:T(8,128)}, f32[64,1024]{1,0:T(8,128)}, f32[64,1024]{1,0:T(8,128)}, /*index=5*...) all-reduce(f32[256]{0:T(256)S(1)} %get-tuple-element.60, ...), channel_id=1, replica_groups=mesh['dp'=4,'seq'=8] {'seq'}, use_global_device_ids=true, to_apply=%region_15.16 | all-reduce | flops 2949632 | bytes 17698816 | tf_op jit(solution)/shard_map/psum | solution.py:307
  (252 shorter events, 196.0 us)
Async XLA Ops:
  7.2 32.0 %all-gather.12.cloned.1.call-start = ((), (), s32[]{:S(2)}) async-start(), calls=%async_computation.10 | async-start | bytes 1310720 | tf_op jit(solution)/shard_map/all_gather | solution.py:60
  7.9 82.7 %all-gather.10.cloned.1.call-start = ((), (), s32[]{:S(2)}) async-start(), calls=%async_computation.9 | async-start | bytes 2621440 | tf_op jit(solution)/shard_map/all_gather | solution.py:59
  8.7 103.6 %all-gather.14.cloned.1.call-start = ((), (), s32[]{:S(2)}) async-start(), calls=%async_computation.11 | async-start | bytes 2359296 | tf_op jit(solution)/shard_map/all_gather | solution.py:125
  41.6 107.2 %all-gather.16.cloned.1.call-start = ((), (), s32[]{:S(2)}) async-start(), calls=%async_computation.12 | async-start | bytes 2621440 | tf_op jit(solution)/shard_map/all_gather | solution.py:63
  42.2 174.1 %all-gather.18.cloned.1.call-start = ((), (), s32[]{:S(2)}) async-start(), calls=%async_computation.13 | async-start | bytes 7208960 | tf_op jit(solution)/shard_map/all_gather | solution.py:65
  42.8 241.1 %all-gather.20.cloned.1.call-start = ((), (), s32[]{:S(2)}) async-start(), calls=%async_computation.14 | async-start | bytes 7208960 | tf_op jit(solution)/shard_map/all_gather | solution.py:66
  43.4 308.2 %all-gather.22.cloned.1.call-start = ((), (), s32[]{:S(2)}) async-start(), calls=%async_computation.15 | async-start | bytes 7208960 | tf_op jit(solution)/shard_map/all_gather | solution.py:67
  44.1 465.2 %reduce-scatter.10.cloned.1.call-start = ((), (), s32[]{:S(2)}) async-start(), calls=%async_computation.16 | async-start | bytes 4718592 | tf_op jit(solution)/shard_map/reduce_scatter | solution.py:239
  151.2 217.6 %copy-start.11 = (f32[256,1024]{1,0:T(8,128)}, f32[256,1024]{1,0:T(8,128)S(1)}, u32[]{:S(2)}) copy-start(f32[256,1024]{1,0:T(8,128)S(1)} %get-tuple-element.54) | copy-start | bytes 3145732
  151.4 132.5 %copy-start.17 = (bf16[256,1024]{1,0:T(8,128)(2,1)}, bf16[256,1024]{1,0:T(8,128)(2,1)S(1)}, u32[]{:S(2)}) copy-start(bf16[256,1024]{1,0:T(8,128)(2,1)S(1)} %multiply_convert_fusion.4) | copy-start | bytes 1572868
  222.2 129.3 %copy-start.31 = (bf16[1,4,64,1024]{3,2,1,0:T(8,128)(2,1)S(1)}, bf16[1,4,64,1024]{3,2,1,0:T(8,128)(2,1)}, u32[]{:S(2)}) copy-start(bf16[1,4,64,1024]{3,2,1,0:T(8,128)(2,1)} %param.24) | copy-start | bytes 1572868
  459.1 81.7 %reduce-scatter.18.cloned.1.call-start = ((), (), s32[]{:S(2)}) async-start(), calls=%async_computation.20 | async-start | bytes 655360 | tf_op jit(solution)/shard_map/reduce_scatter | solution.py:288
  464.8 98.0 %reduce-scatter.16.cloned.1.call-start = ((), (), s32[]{:S(2)}) async-start(), calls=%async_computation.19 | async-start | bytes 655360 | tf_op jit(solution)/shard_map/reduce_scatter | solution.py:285
  477.9 123.7 %reduce-scatter.20.cloned.1.call-start = ((), (), s32[]{:S(2)}) async-start(), calls=%async_computation.21 | async-start | bytes 2621440 | tf_op jit(solution)/shard_map/reduce_scatter | solution.py:291
  480.0 160.5 %reduce-scatter.12.cloned.1.call-start = ((), (), s32[]{:S(2)}) async-start(), calls=%async_computation.17 | async-start | bytes 2621440 | tf_op jit(solution)/shard_map/reduce_scatter | solution.py:279
  485.6 185.5 %reduce-scatter.14.cloned.1.call-start = ((), (), s32[]{:S(2)}) async-start(), calls=%async_computation.18 | async-start | bytes 1310720 | tf_op jit(solution)/shard_map/reduce_scatter | solution.py:282
  511.9 228.3 %reduce-scatter.22.cloned.1.call-start = ((), (), s32[]{:S(2)}) async-start(), calls=%async_computation.22 | async-start | bytes 7208960 | tf_op jit(solution)/shard_map/reduce_scatter | solution.py:297
  517.8 291.3 %reduce-scatter.24.cloned.1.call-start = ((), (), s32[]{:S(2)}) async-start(), calls=%async_computation.23 | async-start | bytes 7208960 | tf_op jit(solution)/shard_map/reduce_scatter | solution.py:300
  523.4 354.6 %reduce-scatter.26.cloned.1.call-start = ((), (), s32[]{:S(2)}) async-start(), calls=%async_computation.24 | async-start | bytes 7208960 | tf_op jit(solution)/shard_map/reduce_scatter | solution.py:303
  535.3 105.2 %copy-start.47 = (f32[256]{0:T(256)S(1)}, f32[256]{0:T(256)}, u32[]{:S(2)}) copy-start(f32[256]{0:T(256)} %copy-done.46) | copy-start | bytes 3076
  535.3 107.4 %copy-start.51 = (bf16[1024]{0:T(1024)(128)(2,1)S(1)}, bf16[1024]{0:T(1024)(128)(2,1)}, u32[]{:S(2)}) copy-start(bf16[1024]{0:T(1024)(128)(2,1)} %get-tuple-element.12) | copy-start | bytes 6148
  535.3 116.4 %copy-start.49 = (f32[256]{0:T(256)S(1)}, f32[256]{0:T(256)}, u32[]{:S(2)}) copy-start(f32[256]{0:T(256)} %copy-done.48) | copy-start | bytes 3076
  540.9 337.1 %copy-start.42 = (bf16[64,1024]{1,0:T(8,128)(2,1)S(1)}, bf16[64,1024]{1,0:T(8,128)(2,1)}, u32[]{:S(2)}) copy-start(bf16[64,1024]{1,0:T(8,128)(2,1)} %reduce-scatter.18.cloned.1.call-done) | copy-start | bytes 393220
  562.8 315.2 %copy-start.43 = (bf16[64,1024]{1,0:T(8,128)(2,1)S(1)}, bf16[64,1024]{1,0:T(8,128)(2,1)}, u32[]{:S(2)}) copy-start(bf16[64,1024]{1,0:T(8,128)(2,1)} %reduce-scatter.16.cloned.1.call-done) | copy-start | bytes 393220
  (51 other events, 615.3 us)
Sparse Core Ops, SparseCore 0:
  9.9 29.3 all-gather.11
  41.1 39.8 all-gather.9
  83.1 29.1 all-gather.13
  113.9 34.8 all-gather.15
  150.5 65.7 all-gather.17
  218.0 65.7 all-gather.19
  285.7 65.7 all-gather.21
  459.3 50.0 reduce-scatter.9
  512.1 22.9 reduce-scatter.17
  538.0 24.7 reduce-scatter.15
  566.4 35.1 reduce-scatter.19
  605.3 35.1 reduce-scatter.11
  643.4 27.7 reduce-scatter.13
  674.3 65.8 reduce-scatter.21
  743.2 65.7 reduce-scatter.23
  812.2 65.7 reduce-scatter.25
where the time goes:
time: 1130 us; the launch traced here: 1120 us
  waiting for transfers between devices  584 us (52%)
  blocking collectives  289 us (26%)
  matrix products  145 us (13%)
  local copies, waits for them, and re-layouts  51.7 us (5%)
  other arithmetic  26.2 us (2%)
  between operations  23.8 us (2%)
    psum x1, blocking collectives, per_device(): lax.psum((shares[0], shares[1], shares[2], shares[3], shares[4], shares[5...  236 us
    reduce_scatter x1, waiting for transfers between devices, per_device(): lax.psum_scatter(grads[7].astype(jnp.bfloat16), 'dp', scatter_dimension=0...  69 us
    reduce_scatter x1, waiting for transfers between devices, per_device(): lax.psum_scatter(grads[9].astype(jnp.bfloat16), 'dp', scatter_dimension=0...  68.9 us
    reduce_scatter x1, waiting for transfers between devices, per_device(): lax.psum_scatter(grads[8].astype(jnp.bfloat16), 'dp', scatter_dimension=0...  68.9 us
    all_gather x1, waiting for transfers between devices, per_device(): lax.all_gather(w_gate, 'dp', axis=0, tiled=True)  64.9 us
    all_gather x1, waiting for transfers between devices, per_device(): lax.all_gather(w_down, 'dp', axis=0, tiled=True)  61.8 us
    all_gather x1, waiting for transfers between devices, per_device(): lax.all_gather(w_up, 'dp', axis=0, tiled=True)  61.7 us
    reduce_scatter x1, waiting for transfers between devices, per_device(): lax.psum_scatter(grads[1].astype(jnp.bfloat16), 'dp', scatter_dimension=0...  38.9 us
  transfers between devices with their start and end apart: 16, of which 14 were waited for; matrix products, arithmetic and copies ran while one was open for 10% of the time, Pallas kernels for 0%

commit v1 on v0

--- a/solution.py
+++ b/solution.py
@@ -54,6 +54,15 @@
     out_grad,
     seq_lengths,
 ):
+    follow_digits_in = lambda axis_id, sample: jnp.concatenate(
+        lax.all_to_all(
+            jnp.stack([sample for _ in range(lax.axis_size(axis_id))], axis=0),
+            concat_axis=0,
+            axis_name=axis_id,
+            split_axis=0,
+        ),
+        axis=0,
+    )
     gathered = (
         lax.all_gather(norm1_gain, "dp", axis=0, tiled=True),
         lax.all_gather(w_query, "dp", axis=0, tiled=True),
@@ -62,7 +71,7 @@
         lax.all_gather(w_value_up, "dp", axis=0, tiled=True),
         lax.all_gather(w_out, "dp", axis=0, tiled=True),
         lax.all_gather(norm2_gain, "dp", axis=0, tiled=True),
-        lax.all_gather(w_gate, "dp", axis=0, tiled=True),
+        follow_digits_in("dp", w_gate),
         lax.all_gather(w_up, "dp", axis=0, tiled=True),
         lax.all_gather(w_down, "dp", axis=0, tiled=True),
     )

time: 1130 us -> 1110 us (0.982)
  waiting for transfers between devices: 584 us -> 493 us
  blocking collectives: 289 us -> 354 us
    all_gather x1, blocking collectives: 14 us -> 82.4 us  [per_device(): lax.all_gather(w_key_up, 'dp', axis=0, tiled=True)]
    all_gather x1 -> x0, waiting for transfers between devices: 64.9 us -> none  [per_device(): lax.all_gather(w_gate, 'dp', axis=0, tiled=True)]
    all_gather x1, waiting for transfers between devices: 18 us -> 0.02 us  [per_device(): lax.all_gather(latent_pieces, 'seq', axis=1, tiled=True)]
  transfers between devices with their start and end apart: 16 -> 16, of which waited for: 14 -> 12; matrix products, arithmetic and copies ran while one was open for 10% -> 10% of each run, Pallas kernels for 0% -> 0%
where the time goes in v1:
time: 1110 us; the launch traced here: 1100 us
  waiting for transfers between devices  493 us (44%)
  blocking collectives  354 us (32%)
  matrix products  145 us (13%)
  local copies, waits for them, and re-layouts  55.4 us (5%)
  other arithmetic  26.3 us (2%)
  between operations  23.8 us (2%)
    psum x1, blocking collectives, per_device(): lax.psum((shares[0], shares[1], shares[2], shares[3], shares[4], shares[5...  236 us
    all_gather x1, blocking collectives, per_device(): lax.all_gather(w_key_up, 'dp', axis=0, tiled=True)  82.4 us
    reduce_scatter x1, waiting for transfers between devices, per_device(): lax.psum_scatter(grads[7].astype(jnp.bfloat16), 'dp', scatter_dimension=0...  69.1 us
    reduce_scatter x1, waiting for transfers between devices, per_device(): lax.psum_scatter(grads[8].astype(jnp.bfloat16), 'dp', scatter_dimension=0...  68.9 us
    reduce_scatter x1, waiting for transfers between devices, per_device(): lax.psum_scatter(grads[9].astype(jnp.bfloat16), 'dp', scatter_dimension=0...  68.9 us
    all_gather x1, waiting for transfers between devices, per_device(): lax.all_gather(w_down, 'dp', axis=0, tiled=True)  61.7 us
    all_gather x1, waiting for transfers between devices, per_device(): lax.all_gather(w_up, 'dp', axis=0, tiled=True)  58.7 us
    reduce_scatter x1, waiting for transfers between devices, per_device(): lax.psum_scatter(grads[1].astype(jnp.bfloat16), 'dp', scatter_dimension=0...  39 us
  transfers between devices with their start and end apart: 16, of which 12 were waited for; matrix products, arithmetic and copies ran while one was open for 10% of the time, Pallas kernels for 0%

profile of v1, /device:TPU:0, one launch (start us, length us, event | category | flops | bytes accessed | tf_op | source)
XLA Modules:
  0.0 1104.0 jit_solution(16555868787294143053)
XLA Ops:
  11.3 9.5 all-gather
  22.6 16.6 %all-gather.11.cloned.1.call-done = bf16[1024,512]{1,0:T(8,128)(2,1)} async-done(((bf16[256,512]{1,0:T(8,128)(2,1)}), bf16[1024,512]{1,0:T(8,128)(2,1)}) %all-gather.11.cloned.1.call-update) | async-done | bytes 1048592 | tf_op jit(solution)/shard_map/all_gather | solution.py:69
  53.8 82.4 %all_gather.33 = bf16[256,1024]{1,0:T(8,128)(2,1)S(1)} all-gather(bf16[64,1024]{1,0:T(8,128)(2,1)S(1)} %copy-done.41), channel_id=1, replica_groups=mesh['dp'=4,'seq'=8] {'dp'}, dimensions={0}, use_global_device_ids=true | all-gather | bytes 655360 | tf_op jit(solution)/shard_map/all_gather | solution.py:70
  136.7 9.4 all_gather.36
  152.6 8.2 all-gather.1
  208.7 58.7 %all-gather.17.cloned.1.call-done = bf16[1024,2816]{1,0:T(8,128)(2,1)} async-done(((bf16[256,2816]{1,0:T(8,128)(2,1)}), bf16[1024,2816]{1,0:T(8,128)(2,1)}) %all-gather.17.cloned.1.call-update) | async-done | bytes 5767184 | tf_op jit(solution)/shard_map/all_gather | solution.py:75
  273.2 61.7 %all-gather.19.cloned.1.call-done = bf16[2816,1024]{1,0:T(8,128)(2,1)} async-done(((bf16[704,1024]{1,0:T(8,128)(2,1)}), bf16[2816,1024]{1,0:T(8,128)(2,1)}) %all-gather.19.cloned.1.call-update) | async-done | bytes 5767184 | tf_op jit(solution)/shard_map/all_gather | solution.py:76
  334.9 9.5 multiply_convert_fusion.2
  361.3 6.8 multiply_convert_fusion
  374.3 8.1 bitcast_add_fusion
  394.8 7.5 bitcast_add_fusion.1
  407.7 6.7 dynamic_update_slice.12
  417.2 6.5 dynamic_update_slice.13
  435.8 6.6 dynamic_update_slice.15
  468.9 23.6 %reduce-scatter.10.cloned.1.call-done = f32[4,64,512]{2,1,0:T(8,128)} async-done(((f32[4,512,512]{2,1,0:T(8,128)}), f32[4,64,512]{2,1,0:T(8,128)}) %reduce-scatter.10.cloned.1.call-update) | async-done | bytes 524304 | tf_op jit(solution)/shard_map/reduce_scatter | solution.py:248
  524.2 22.0 %reduce-scatter.16.cloned.1.call-done = bf16[64,1024]{1,0:T(8,128)(2,1)} async-done(((bf16[256,1024]{1,0:T(8,128)(2,1)}), bf16[64,1024]{1,0:T(8,128)(2,1)}) %reduce-scatter.16.cloned.1.call-update) | async-done | bytes 131088 | tf_op jit(solution)/shard_map/reduce_scatter | solution.py:294
  546.2 38.6 %reduce-scatter.20.cloned.1.call-done = bf16[256,1024]{1,0:T(8,128)(2,1)} async-done(((bf16[1024,1024]{1,0:T(8,128)(2,1)}), bf16[256,1024]{1,0:T(8,128)(2,1)}) %reduce-scatter.20.cloned.1.call-update) | async-done | bytes 524304 | tf_op jit(solution)/shard_map/reduce_scatter | solution.py:300
  584.8 39.0 %reduce-scatter.12.cloned.1.call-done = bf16[256,1024]{1,0:T(8,128)(2,1)} async-done(((bf16[1024,1024]{1,0:T(8,128)(2,1)}), bf16[256,1024]{1,0:T(8,128)(2,1)}) %reduce-scatter.12.cloned.1.call-update) | async-done | bytes 524304 | tf_op jit(solution)/shard_map/reduce_scatter | solution.py:288
  626.0 8.9 all-reduce.3
  636.2 18.1 %reduce-scatter.14.cloned.1.call-done = bf16[256,512]{1,0:T(8,128)(2,1)} async-done(((bf16[1024,512]{1,0:T(8,128)(2,1)}), bf16[256,512]{1,0:T(8,128)(2,1)}) %reduce-scatter.14.cloned.1.call-update) | async-done | bytes 262160 | tf_op jit(solution)/shard_map/reduce_scatter | solution.py:291
  654.3 69.1 %reduce-scatter.22.cloned.1.call-done = bf16[256,2816]{1,0:T(8,128)(2,1)} async-done(((bf16[1024,2816]{1,0:T(8,128)(2,1)}), bf16[256,2816]{1,0:T(8,128)(2,1)}) %reduce-scatter.22.cloned.1.call-update) | async-done | bytes 1441808 | tf_op jit(solution)/shard_map/reduce_scatter | solution.py:306
  723.4 68.9 %reduce-scatter.24.cloned.1.call-done = bf16[256,2816]{1,0:T(8,128)(2,1)} async-done(((bf16[1024,2816]{1,0:T(8,128)(2,1)}), bf16[256,2816]{1,0:T(8,128)(2,1)}) %reduce-scatter.24.cloned.1.call-update) | async-done | bytes 1441808 | tf_op jit(solution)/shard_map/reduce_scatter | solution.py:309
  792.4 68.9 %reduce-scatter.26.cloned.1.call-done = bf16[704,1024]{1,0:T(8,128)(2,1)} async-done(((bf16[2816,1024]{1,0:T(8,128)(2,1)}), bf16[704,1024]{1,0:T(8,128)(2,1)}) %reduce-scatter.26.cloned.1.call-update) | async-done | bytes 1441808 | tf_op jit(solution)/shard_map/reduce_scatter | solution.py:312
  861.3 235.7 %all-reduce.5 = (f32[256]{0:T(256)}, f32[256,1024]{1,0:T(8,128)}, f32[256,512]{1,0:T(8,128)}, f32[64,1024]{1,0:T(8,128)}, f32[64,1024]{1,0:T(8,128)}, /*index=5*...) all-reduce(f32[256]{0:T(256)S(1)} %get-tuple-element.60, ...), channel_id=1, replica_groups=mesh['dp'=4,'seq'=8] {'seq'}, use_global_device_ids=true, to_apply=%region_15.16 | all-reduce | flops 2949632 | bytes 17698816 | tf_op jit(solution)/shard_map/psum | solution.py:316
  (254 shorter events, 189.1 us)
Async XLA Ops:
  7.2 32.0 %all-gather.11.cloned.1.call-start = ((), (), s32[]{:S(2)}) async-start(), calls=%async_computation.11 | async-start | bytes 1310720 | tf_op jit(solution)/shard_map/all_gather | solution.py:69
  7.9 155.5 %all-gather.9.cloned.1.call-start = ((), (), s32[]{:S(2)}) async-start(), calls=%async_computation.10 | async-start | bytes 2621440 | tf_op jit(solution)/shard_map/all_gather | solution.py:68
  8.7 158.2 %all-gather.13.cloned.1.call-start = ((), (), s32[]{:S(2)}) async-start(), calls=%async_computation.12 | async-start | bytes 2359296 | tf_op jit(solution)/shard_map/all_gather | solution.py:134
  41.6 158.2 %all-gather.15.cloned.1.call-start = ((), (), s32[]{:S(2)}) async-start(), calls=%async_computation.13 | async-start | bytes 2621440 | tf_op jit(solution)/shard_map/all_gather | solution.py:72
  42.2 225.2 %all-gather.17.cloned.1.call-start = ((), (), s32[]{:S(2)}) async-start(), calls=%async_computation.14 | async-start | bytes 7208960 | tf_op jit(solution)/shard_map/all_gather | solution.py:75
  45.6 156.8 %all-to-all-start = ((bf16[4,256,2816]{2,1,0:T(8,128)(2,1)}), bf16[4,256,2816]{2,1,0:T(8,128)(2,1)}, u32[]{:S(2)}, u32[]{:S(2)}) async-start(bf16[4,256,2816]{2,1,0:T(8,128)(2,1)} %stack.32), calls=%async_computation | async-start | bytes 11534336 | tf_op jit(solution)/shard_map/all_to_all | solution.py:58
  51.0 101.5 %copy-start.55 = (bf16[256]{0:T(256)(128)(2,1)S(1)}, bf16[256]{0:T(256)(128)(2,1)}, u32[]{:S(2)}) copy-start(bf16[256]{0:T(256)(128)(2,1)} %param.20) | copy-start | bytes 1540
  51.1 283.8 %all-gather.19.cloned.1.call-start = ((), (), s32[]{:S(2)}) async-start(), calls=%async_computation.15 | async-start | bytes 7208960 | tf_op jit(solution)/shard_map/all_gather | solution.py:76
  51.6 440.9 %reduce-scatter.10.cloned.1.call-start = ((), (), s32[]{:S(2)}) async-start(), calls=%async_computation.16 | async-start | bytes 4718592 | tf_op jit(solution)/shard_map/reduce_scatter | solution.py:248
  202.3 150.0 %copy-start.11 = (f32[256,1024]{1,0:T(8,128)}, f32[256,1024]{1,0:T(8,128)S(1)}, u32[]{:S(2)}) copy-start(f32[256,1024]{1,0:T(8,128)S(1)} %get-tuple-element.54) | copy-start | bytes 3145732
  208.7 126.2 %copy-start.31 = (bf16[1,4,64,1024]{3,2,1,0:T(8,128)(2,1)S(1)}, bf16[1,4,64,1024]{3,2,1,0:T(8,128)(2,1)}, u32[]{:S(2)}) copy-start(bf16[1,4,64,1024]{3,2,1,0:T(8,128)(2,1)} %param.24) | copy-start | bytes 1572868
  442.4 81.8 %reduce-scatter.18.cloned.1.call-start = ((), (), s32[]{:S(2)}) async-start(), calls=%async_computation.20 | async-start | bytes 655360 | tf_op jit(solution)/shard_map/reduce_scatter | solution.py:297
  448.0 98.2 %reduce-scatter.16.cloned.1.call-start = ((), (), s32[]{:S(2)}) async-start(), calls=%async_computation.19 | async-start | bytes 655360 | tf_op jit(solution)/shard_map/reduce_scatter | solution.py:294
  461.1 123.6 %reduce-scatter.20.cloned.1.call-start = ((), (), s32[]{:S(2)}) async-start(), calls=%async_computation.21 | async-start | bytes 2621440 | tf_op jit(solution)/shard_map/reduce_scatter | solution.py:300
  463.3 160.6 %reduce-scatter.12.cloned.1.call-start = ((), (), s32[]{:S(2)}) async-start(), calls=%async_computation.17 | async-start | bytes 2621440 | tf_op jit(solution)/shard_map/reduce_scatter | solution.py:288
  468.8 185.5 %reduce-scatter.14.cloned.1.call-start = ((), (), s32[]{:S(2)}) async-start(), calls=%async_computation.18 | async-start | bytes 1310720 | tf_op jit(solution)/shard_map/reduce_scatter | solution.py:291
  495.1 228.3 %reduce-scatter.22.cloned.1.call-start = ((), (), s32[]{:S(2)}) async-start(), calls=%async_computation.22 | async-start | bytes 7208960 | tf_op jit(solution)/shard_map/reduce_scatter | solution.py:306
  501.0 291.4 %reduce-scatter.24.cloned.1.call-start = ((), (), s32[]{:S(2)}) async-start(), calls=%async_computation.23 | async-start | bytes 7208960 | tf_op jit(solution)/shard_map/reduce_scatter | solution.py:309
  506.7 354.7 %reduce-scatter.26.cloned.1.call-start = ((), (), s32[]{:S(2)}) async-start(), calls=%async_computation.24 | async-start | bytes 7208960 | tf_op jit(solution)/shard_map/reduce_scatter | solution.py:312
  518.6 105.3 %copy-start.48 = (f32[256]{0:T(256)S(1)}, f32[256]{0:T(256)}, u32[]{:S(2)}) copy-start(f32[256]{0:T(256)} %copy-done.47) | copy-start | bytes 3076
  518.6 107.4 %copy-start.52 = (bf16[1024]{0:T(1024)(128)(2,1)S(1)}, bf16[1024]{0:T(1024)(128)(2,1)}, u32[]{:S(2)}) copy-start(bf16[1024]{0:T(1024)(128)(2,1)} %get-tuple-element.12) | copy-start | bytes 6148
  518.6 116.5 %copy-start.50 = (f32[256]{0:T(256)S(1)}, f32[256]{0:T(256)}, u32[]{:S(2)}) copy-start(f32[256]{0:T(256)} %copy-done.49) | copy-start | bytes 3076
  524.2 337.2 %copy-start.43 = (bf16[64,1024]{1,0:T(8,128)(2,1)S(1)}, bf16[64,1024]{1,0:T(8,128)(2,1)}, u32[]{:S(2)}) copy-start(bf16[64,1024]{1,0:T(8,128)(2,1)} %reduce-scatter.18.cloned.1.call-done) | copy-start | bytes 393220
  546.2 315.1 %copy-start.44 = (bf16[64,1024]{1,0:T(8,128)(2,1)S(1)}, bf16[64,1024]{1,0:T(8,128)(2,1)}, u32[]{:S(2)}) copy-start(bf16[64,1024]{1,0:T(8,128)(2,1)} %reduce-scatter.16.cloned.1.call-done) | copy-start | bytes 393220
  (52 other events, 500.8 us)
Sparse Core Ops, SparseCore 0:
  9.9 29.3 all-gather.10
  41.1 80.4 all-gather.8
  123.8 39.4 all-gather.12
  165.0 34.7 all-gather.14
  201.5 65.7 all-gather.16
  269.1 65.7 all-gather.18
  442.5 50.0 reduce-scatter.9
  495.4 22.9 reduce-scatter.17
  521.4 24.7 reduce-scatter.15
  549.6 35.1 reduce-scatter.19
  588.6 35.1 reduce-scatter.11
  626.6 27.6 reduce-scatter.13
  657.6 65.8 reduce-scatter.21
  726.6 65.7 reduce-scatter.23
  795.5 65.7 reduce-scatter.25
